TPU v7x, 256 devices: a whole 4x4x8 slice. The times are simulated.
256 devices in a mesh: cfg: 8 (over y, core), node: 32 (over z, x).
Axes of the slice: x: 4, y: 4, z: 8, core: 2. Of those that a mesh axis runs over, the one named last changes fastest.
Arguments:
- node_feats: bfloat16 [1048576, 256], P(('cfg', 'node')), may hold values from -6 to 6
- neighbors: int32 [1048576, 4], P(('cfg', 'node')), may hold values from 0 to 5119
- self_weight: bfloat16 [256, 256], replicated, may hold values from -0.375 to 0.375
- neighbor_weight: bfloat16 [256, 256], replicated, may hold values from -0.375 to 0.375
- sage_bias: float32 [256], replicated, may hold values from -3 to 3
- conf_index: int32 [32768], P(('cfg', 'node')), may hold values from 0 to 4095
- layout_ids: int32 [128, 32768], P('cfg', 'node'), may hold values from 0 to 127
- join_weight: bfloat16 [256, 256], replicated, may hold values from -0.375 to 0.375
- layout_table: bfloat16 [128, 256], replicated, may hold values from -6 to 6
- join_bias: float32 [256], replicated, may hold values from -3 to 3
- mid_weight: bfloat16 [256, 256], replicated, may hold values from -0.375 to 0.375
- mid_bias: float32 [256], replicated, may hold values from -3 to 3
- score_weight: float32 [256], replicated, may hold values from -0.375 to 0.375
- config_pairs: int32 [512, 2], replicated, may hold values from 0 to 127
Outputs:
- node_embed: bfloat16 [1048576, 256], P(('cfg', 'node'))
- pair_loss: float32 [], replicated
- conf_grad: float32 [32768, 256], P(('cfg', 'node'))
All inputs are finite; a program needn't handle non-finite values.
Results may differ from a plain program's by a relative error of at most 0.028.
Values may be sent and summed in bfloat16 or wider, within the bound.
No kernel may reach another device: no remote copies, remote signals or barrier semaphores. Data moves between devices by JAX's collectives and lax.ppermute only.
A program may use at most 64 MiB of HBM per device.

v0:
```python
import math
import jax
import jax.numpy as jnp
from jax import lax
from jax.sharding import PartitionSpec as P

HALO = 512


def with_halo(value, sides, width):
    for axis, dim in sides:
        size, length = (lax.axis_size(axis), value.shape[dim])
        up = [(i, (i + 1) % size) for i in range(size - 1)]
        down = [(j, i) for i, j in up]
        last = lax.slice_in_dim(value, length - width, length, axis=dim)
        leading = lax.slice_in_dim(value, 0, width, axis=dim)
        before = lax.ppermute(last, axis, up)
        after = lax.ppermute(leading, axis, down)
        value = jnp.concatenate([before, value, after], axis=dim)
    return value


def silu_slope(value):
    sigma = jax.nn.sigmoid(value)
    return sigma * (1.0 + value * (1.0 - sigma))


def pair_terms(config_score, config_pairs):
    config_total_count = config_score.shape[0]
    pair_first = config_pairs[:, 0]
    pair_second = config_pairs[:, 1]
    score_gap = jnp.take(config_score, pair_second) - jnp.take(config_score, pair_first)
    pair_loss = jnp.mean(jax.nn.softplus(score_gap))
    pair_slope = jax.nn.sigmoid(score_gap) / config_pairs.shape[0]
    columns = jnp.arange(config_total_count, dtype=jnp.int32)
    signed = (pair_second[:, None] == columns[None, :]).astype(jnp.float32) - (
        pair_first[:, None] == columns[None, :]
    ).astype(jnp.float32)
    score_grad = 65536.0 * jnp.dot(pair_slope, signed, precision=lax.Precision.HIGHEST)
    return (pair_loss, score_grad)


def shards(
    node_feats,
    neighbors,
    self_weight,
    neighbor_weight,
    sage_bias,
    conf_index,
    layout_ids,
    join_weight,
    layout_table,
    join_bias,
    mid_weight,
    mid_bias,
    score_weight,
    config_pairs,
):
    node_rows = node_feats.shape[0]
    feat_width = node_feats.shape[1]
    hidden_width = join_weight.shape[1]
    padded = with_halo(node_feats, ((("cfg", "node"), 0),), HALO)
    summed = jnp.zeros((node_rows, feat_width), jnp.float32)
    for neighbor in range(neighbors.shape[1]):
        summed = summed + jnp.take(padded, neighbors[:, neighbor], axis=0).astype(jnp.float32)
    neighbour_mean = (summed / neighbors.shape[1]).astype(jnp.bfloat16)
    pre_act = (
        jnp.dot(node_feats, self_weight, preferred_element_type=jnp.float32)
        + jnp.dot(neighbour_mean, neighbor_weight, preferred_element_type=jnp.float32)
        + sage_bias
    )
    node_embed = jax.nn.silu(pre_act).astype(jnp.bfloat16)
    conf_src = jnp.take(node_embed, conf_index, axis=0)
    node_count = lax.axis_size("node")
    group_count = lax.axis_size("cfg")
    local_conf = conf_index.shape[0]
    per_peer = local_conf // node_count
    local_configs = layout_ids.shape[0]
    norm_scale = 1.0 / math.sqrt(layout_ids.shape[1] * node_count)
    table_ids = jnp.arange(layout_table.shape[0], dtype=jnp.int32)

    def hidden_rows(base_rows, row_ids):
        picks = (row_ids[:, None] == table_ids[None, :]).astype(jnp.bfloat16)
        inner_pre = (
            base_rows + jnp.dot(picks, layout_table, preferred_element_type=jnp.float32) + join_bias
        )
        inner_act = jax.nn.silu(inner_pre).astype(jnp.bfloat16)
        outer_pre = jnp.dot(inner_act, mid_weight, preferred_element_type=jnp.float32) + mid_bias
        return (inner_pre, outer_pre)

    grouped = lax.all_gather(conf_src, "cfg", axis=0, tiled=True)
    spread = lax.all_to_all(
        grouped.reshape(group_count, node_count, per_peer, feat_width),
        "node",
        split_axis=1,
        concat_axis=1,
        tiled=True,
    )
    conf_rows = spread.reshape(-1, feat_width)
    row_count = conf_rows.shape[0]
    base = jnp.dot(conf_rows, join_weight, preferred_element_type=jnp.float32)

    def config_total(row_ids):
        inner_pre, outer_pre = hidden_rows(base, row_ids)
        scores = jnp.dot(jax.nn.silu(outer_pre), score_weight, precision=lax.Precision.HIGHEST)
        return jnp.sum(scores)

    partial_sums = lax.map(config_total, layout_ids)
    local_score = lax.psum(partial_sums, "node") * norm_scale
    config_score = lax.all_gather(local_score, "cfg", axis=0, tiled=True)
    pair_loss, score_grad = pair_terms(config_score, config_pairs)
    local_grads = lax.dynamic_slice_in_dim(
        score_grad, lax.axis_index("cfg") * local_configs, local_configs, 0
    )

    def config_step(carried, inputs):
        row_ids, config_grad = inputs
        inner_pre, outer_pre = hidden_rows(base, row_ids)
        outer_grad = (config_grad * norm_scale * score_weight * silu_slope(outer_pre)).astype(
            jnp.bfloat16
        )
        inner_grad = lax.dot_general(
            outer_grad, mid_weight, (((1,), (1,)), ((), ())), preferred_element_type=jnp.float32
        ) * silu_slope(inner_pre)
        return (carried + inner_grad, None)

    zero_rows = jnp.zeros((row_count, hidden_width), jnp.float32)
    group_part, unused = lax.scan(config_step, zero_rows, (layout_ids, local_grads))
    row_sum = lax.psum_scatter(
        group_part.astype(jnp.bfloat16), "cfg", scatter_dimension=0, tiled=True
    )
    local_grad = lax.dot_general(
        row_sum, join_weight, (((1,), (1,)), ((), ())), preferred_element_type=jnp.float32
    )
    returned = lax.all_to_all(
        local_grad.reshape(node_count, per_peer, feat_width).astype(jnp.bfloat16),
        "node",
        split_axis=0,
        concat_axis=0,
        tiled=True,
    ).astype(jnp.float32)
    conf_grad = returned.reshape(-1, feat_width)
    return (node_embed, pair_loss, conf_grad)


def solution(mesh):
    placed = (
        P(("cfg", "node"), None),
        P(("cfg", "node"), None),
        P(),
        P(),
        P(),
        P(("cfg", "node")),
        P("cfg", "node"),
        P(),
        P(),
        P(),
        P(),
        P(),
        P(),
        P(),
    )
    return jax.shard_map(
        shards,
        mesh=mesh,
        in_specs=placed,
        out_specs=(P(("cfg", "node"), None), P(), P(("cfg", "node"), None)),
        check_vma=False,
    )
```

profile of v0, /device:TPU:2, one launch (start us, length us, event | category | flops | bytes accessed | tf_op | source)
XLA Modules:
  0.0 480.4 jit_solution(4784900319033597347)
XLA Ops:
  8.3 3.4 collective-permute-start
  16.6 4.4 fusion.62
  21.4 17.0 %gather_fusion.4 = bf16[4096,256]{1,0:T(8,128)(2,1)} fusion(bf16[5120,256]{1,0:T(8,128)(2,1)S(1)} %constant_dynamic-update-slice_fusion, s32[4096]{0:T(1024)S(1)} %fusion.55), kind=kCustom, calls=%fused_computation.4.clone | custom fusion | bytes 4210688 | tf_op jit(solution)/shard_map/jit(_take)/gather | solution.py:65
  38.4 16.9 %gather_fusion.1 = bf16[4096,256]{1,0:T(8,128)(2,1)} fusion(bf16[5120,256]{1,0:T(8,128)(2,1)S(1)} %constant_dynamic-update-slice_fusion, s32[4096]{0:T(1024)S(1)} %fusion.52), kind=kCustom, calls=%fused_computation.clone | custom fusion | bytes 4210688 | tf_op jit(solution)/shard_map/jit(_take)/gather | solution.py:65
  55.3 16.9 %gather_fusion.2 = bf16[4096,256]{1,0:T(8,128)(2,1)} fusion(bf16[5120,256]{1,0:T(8,128)(2,1)S(1)} %constant_dynamic-update-slice_fusion, s32[4096]{0:T(1024)S(1)} %fusion.53), kind=kCustom, calls=%fused_computation.2.clone | custom fusion | bytes 4210688 | tf_op jit(solution)/shard_map/jit(_take)/gather | solution.py:65
  72.2 16.9 %gather_fusion.3 = bf16[4096,256]{1,0:T(8,128)(2,1)} fusion(bf16[5120,256]{1,0:T(8,128)(2,1)S(1)} %constant_dynamic-update-slice_fusion, s32[4096]{0:T(1024)S(1)} %fusion.54), kind=kCustom, calls=%fused_computation.3.clone | custom fusion | bytes 4210688 | tf_op jit(solution)/shard_map/jit(_take)/gather | solution.py:65
  89.1 8.0 %multiply_convert_fusion.5 = bf16[4096,256]{1,0:T(8,128)(2,1)S(1)} fusion(f32[4096,256]{1,0:T(8,128)} %fusion.62, bf16[256,256]{1,0:T(8,128)(2,1)S(1)} %copy-done.8, bf16[4096,256]{1,0:T(8,128)(2,1)} %gather_fusion.4, bf16[4096,256]{1,0:T(8,128)(2,1)} %gather_fusion.3, bf16[4096,256]{1,0:T(8,128)(2,1)} %gather_fusion.2, ...), kind=kOutput, calls=%fused_computation.48 | convolution fusion | flops 557842432 | bytes 14828544 | tf_op jit(solution)/shard_map/dot_general | solution.py:69
  98.6 13.6 %all_gather.6 = bf16[1024,256]{1,0:T(8,128)(2,1)S(1)} all-gather(bf16[128,256]{1,0:T(8,128)(2,1)S(1)} %broadcast_select_fusion), channel_id=1, replica_groups=mesh['cfg'=8,'node'=32] {'cfg'}, dimensions={0}, use_global_device_ids=true | all-gather | bytes 589824 | tf_op jit(solution)/shard_map/all_gather | solution.py:91
  113.4 13.7 %all-to-all-start = ((bf16[8,32,4,256]{3,2,0,1:T(4,128)(2,1)}), bf16[8,32,4,256]{3,2,0,1:T(4,128)(2,1)S(1)}, u32[]{:S(2)}, u32[]{:S(2)}) async-start(bf16[8,32,4,256]{3,2,0,1:T(4,128)(2,1)} %copy.18), calls=%async_computation | async-start | bytes 1048576 | tf_op jit(solution)/shard_map/all_to_all | solution.py:92
  128.5 15.9 %all-to-all-done = bf16[8,32,4,256]{3,2,0,1:T(4,128)(2,1)S(1)} async-done(((bf16[8,32,4,256]{3,2,0,1:T(4,128)(2,1)}), bf16[8,32,4,256]{3,2,0,1:T(4,128)(2,1)S(1)}, u32[]{:S(2)}, u32[]{:S(2)}) %all-to-all-start) | async-done | bytes 524320 | tf_op jit(solution)/shard_map/all_to_all | solution.py:92
  145.1 113.5 %while.22 = (s32[]{:T(128)}, f32[16]{0:T(128)S(1)}, s32[16,1024]{1,0:T(8,128)}, bf16[128,256]{1,0:T(8,128)(2,1)S(1)}, f32[1024,256]{1,0:T(8,128)S(1)}, /*index=5...) while((s32[]{:T(128)}, f32[16]{0:T(128)S(1)}, ...), condition=%wide.region_2.4_spmd.clone, body=%wide.region_0.3_spmd.clone.sunk | while | flops 207750144 | bytes 3366021 | solution.py:108
  160.1 2.5 convolution_add_fusion.6
  174.3 2.5 convolution_add_fusion.6
  195.6 2.5 convolution_add_fusion.6
  216.8 2.5 convolution_add_fusion.6
  245.2 2.5 convolution_add_fusion.6
  258.7 70.7 %psum.7 = f32[16]{0:T(128)S(1)} all-reduce(f32[16]{0:T(128)S(1)} %get-tuple-element.114), channel_id=1, replica_groups=mesh['cfg'=8,'node'=32] {'node'}, use_global_device_ids=true, to_apply=%region_3.5 | all-reduce | flops 16 | bytes 128 | tf_op jit(solution)/shard_map/psum | solution.py:109
  329.5 12.4 %all-reduce = f32[128]{0:T(128)S(1)} all-reduce(f32[128]{0:T(128)S(1)} %multiply_dynamic-update-slice_fusion), channel_id=1, replica_groups=mesh['cfg'=8,'node'=32] {'cfg'}, use_global_device_ids=true, to_apply=%add | all-reduce | flops 128 | bytes 1024
  341.9 3.3 gather_fusion.5
  345.2 3.3 gather_fusion.6
  349.1 72.5 %while.23 = (s32[]{:T(128)}, f32[1024,256]{1,0:T(8,128)S(1)}, f32[16]{0:T(128)S(1)}, f32[256]{0:T(256)S(1)}, s32[16,1024]{1,0:T(8,128)}, /*index=5*/bf16[128,256...) while((s32[]{:T(128)}, f32[1024,256]{1,0:T(8,128)S(1)}, ...), condition=%wide.region_6.9_spmd.clone, body=%wide.region_5.8_spmd.clone.sunk | while | flops 342753536 | bytes 5457063 | solution.py:128
  422.4 28.7 %reduce-scatter.2.cloned.1.call-done = bf16[128,256]{1,0:T(8,128)(2,1)} async-done(((bf16[1024,256]{1,0:T(8,128)(2,1)}), bf16[128,256]{1,0:T(8,128)(2,1)}) %reduce-scatter.2.cloned.1.call-update) | async-done | bytes 65552 | tf_op jit(solution)/shard_map/reduce_scatter | solution.py:129
  452.8 10.2 %all-to-all-start.1 = ((bf16[32,4,256]{2,1,0:T(4,128)(2,1)}), bf16[32,4,256]{2,1,0:T(4,128)(2,1)S(1)}, u32[]{:S(2)}, u32[]{:S(2)}) async-start(bf16[32,4,256]{2,1,0:T(4,128)(2,1)} %convert_element_type.55), calls=%async_computation.2 | async-start | bytes 131072 | tf_op jit(solution)/shard_map/all_to_all | solution.py:135
  464.3 7.4 %all-to-all-done.1 = bf16[32,4,256]{2,1,0:T(4,128)(2,1)S(1)} async-done(((bf16[32,4,256]{2,1,0:T(4,128)(2,1)}), bf16[32,4,256]{2,1,0:T(4,128)(2,1)S(1)}, u32[]{:S(2)}, u32[]{:S(2)}) %all-to-all-start.1) | async-done | bytes 65568 | tf_op jit(solution)/shard_map/all_to_all | solution.py:135
  (222 shorter events, 176.9 us)
Async XLA Ops:
  7.2 9.4 %copy-start = (bf16[256,256]{1,0:T(8,128)(2,1)S(1)}, bf16[256,256]{1,0:T(8,128)(2,1)}, u32[]{:S(2)}) copy-start(bf16[256,256]{1,0:T(8,128)(2,1)} %param.24) | copy-start | bytes 393220
  8.3 12.8 %collective-permute-start = (bf16[512,256]{1,0:T(8,128)(2,1)S(1)}, bf16[512,256]{1,0:T(8,128)(2,1)S(1)}, u32[]{:S(2)}, u32[]{:S(2)}) collective-permute-start(bf16[512,256]{1,0:T(8,128)(2,1)S(1)} %get-tuple-element.212), channel_id=1, source_target_pairs={{0,1},{1,2},{2,3},{3,4},{4,5},{5,6},{6,7},{7,8},{8,9},{9,10},{10,1... | collective-permute-start | bytes 786440 | tf_op jit(solution)/shard_map/ppermute | solution.py:17
  11.7 9.7 %collective-permute-start.1 = (bf16[512,256]{1,0:T(8,128)(2,1)S(1)}, bf16[512,256]{1,0:T(8,128)(2,1)S(1)}, u32[]{:S(2)}, u32[]{:S(2)}) collective-permute-start(bf16[512,256]{1,0:T(8,128)(2,1)S(1)} %get-tuple-element.211), channel_id=1, source_target_pairs={{1,0},{2,1},{3,2},{4,3},{5,4},{6,5},{7,6},{8,7},{9,8},{10,9},{11,1... | collective-permute-start | bytes 786440 | tf_op jit(solution)/shard_map/ppermute | solution.py:18
  16.6 4.5 copy-start.1
  72.2 16.9 %copy-start.8 = (bf16[256,256]{1,0:T(8,128)(2,1)S(1)}, bf16[256,256]{1,0:T(8,128)(2,1)}, u32[]{:S(2)}) copy-start(bf16[256,256]{1,0:T(8,128)(2,1)} %param.25) | copy-start | bytes 393220
  72.2 16.9 %copy-start.9 = (f32[256]{0:T(256)S(1)}, f32[256]{0:T(256)}, u32[]{:S(2)}) copy-start(f32[256]{0:T(256)} %param.26) | copy-start | bytes 3076
  97.2 1.3 copy-start.4
  97.2 30.0 %copy-start.11 = (u32[256]{0:T(256)S(1)}, u32[256]{0:T(256)}, u32[]{:S(2)}) copy-start(u32[256]{0:T(256)} %constant.97) | copy-start | bytes 3076
  98.5 30.0 %copy-start.7 = (s32[512,2]{0,1:T(2,128)S(1)}, s32[512,2]{0,1:T(2,128)}, u32[]{:S(2)}) copy-start(s32[512,2]{0,1:T(2,128)} %param.35) | copy-start | bytes 12292
  112.4 32.4 %copy-start.3 = (bf16[256,256]{1,0:T(8,128)(2,1)S(1)}, bf16[256,256]{1,0:T(8,128)(2,1)}, u32[]{:S(2)}) copy-start(bf16[256,256]{1,0:T(8,128)(2,1)} %param.29) | copy-start | bytes 393220
  113.4 31.0 %all-to-all-start = ((bf16[8,32,4,256]{3,2,0,1:T(4,128)(2,1)}), bf16[8,32,4,256]{3,2,0,1:T(4,128)(2,1)S(1)}, u32[]{:S(2)}, u32[]{:S(2)}) async-start(bf16[8,32,4,256]{3,2,0,1:T(4,128)(2,1)} %copy.18), calls=%async_computation | async-start | bytes 1048576 | tf_op jit(solution)/shard_map/all_to_all | solution.py:92
  127.1 18.0 %copy-start.2 = (bf16[128,256]{1,0:T(8,128)(2,1)S(1)}, bf16[128,256]{1,0:T(8,128)(2,1)}, u32[]{:S(2)}) copy-start(bf16[128,256]{1,0:T(8,128)(2,1)} %param.30) | copy-start | bytes 196612
  127.1 18.0 %copy-start.5 = (f32[256]{0:T(256)S(1)}, f32[256]{0:T(256)}, u32[]{:S(2)}) copy-start(f32[256]{0:T(256)} %param.31) | copy-start | bytes 3076
  127.1 18.0 %copy-start.6 = (f32[256]{0:T(256)S(1)}, f32[256]{0:T(256)}, u32[]{:S(2)}) copy-start(f32[256]{0:T(256)} %param.34) | copy-start | bytes 3076
  127.1 18.0 %copy-start.10 = (f32[256]{0:T(256)S(1)}, f32[256]{0:T(256)}, u32[]{:S(2)}) copy-start(f32[256]{0:T(256)} %param.33) | copy-start | bytes 3076
  127.2 324.0 %reduce-scatter.2.cloned.1.call-start = ((), (), s32[]{:S(2)}) async-start(), calls=%async_computation.3 | async-start | bytes 589824 | tf_op jit(solution)/shard_map/reduce_scatter | solution.py:129
  452.8 18.9 %all-to-all-start.1 = ((bf16[32,4,256]{2,1,0:T(4,128)(2,1)}), bf16[32,4,256]{2,1,0:T(4,128)(2,1)S(1)}, u32[]{:S(2)}, u32[]{:S(2)}) async-start(bf16[32,4,256]{2,1,0:T(4,128)(2,1)} %convert_element_type.55), calls=%async_computation.2 | async-start | bytes 131072 | tf_op jit(solution)/shard_map/all_to_all | solution.py:135
Sparse Core Ops, SparseCore 0:
  422.5 28.5 reduce-scatter.1
where the time goes:
time: 485 us; the launch traced here: 480 us
  matrix products  132 us (27%)
  local copies, waits for them, and re-layouts  127 us (26%)
  blocking collectives  96.7 us (20%)
  waiting for transfers between devices  52.2 us (11%)
  starting transfers between devices  29.8 us (6%)
  between operations  16.9 us (3%)
  other arithmetic  14 us (3%)
  loops' own time  11.2 us (2%)
    psum x1, blocking collectives, shards(): local_score = lax.psum(partial_sums, 'node') * norm_scale  70.7 us
    gather x4, local copies, waits for them, and re-layouts, shards(): jnp.take(padded, neighbors[:, neighbor], axis=0).astype(jnp.float32)  67.7 us
    dot_general x16, matrix products, hidden_rows(): jnp.dot(inner_act, mid_weight, preferred_element_type=jnp.float32)  40 us
    dot_general x16, matrix products, config_total(): jnp.dot(jax.nn.silu(outer_pre), score_weight, precision=lax.Precision.HIG...  38.7 us
    dot_general x16, matrix products, config_step(): lax.dot_general(outer_grad, mid_weight, (((1,), (1,)), ((), ())), preferr...  33.9 us
    reduce_scatter x1, waiting for transfers between devices, shards(): lax.psum_scatter(group_part.astype(jnp.bfloat16), 'cfg', scatter_dimensio...  28.7 us
    dynamic_slice x32, local copies, waits for them, and re-layouts, shards(): partial_sums = lax.map(config_total, layout_ids)  24.5 us
    all_to_all x1, waiting for transfers between devices, shards(): lax.all_to_all(grouped.reshape(group_count, node_count, per_peer, feat_wi...  15.9 us
  transfers between devices with their start and end apart: 5, of which 4 were waited for; matrix products, arithmetic and copies ran while one was open for 2% of the time, Pallas kernels for 0%

commit v1 on v0

--- a/solution.py
+++ b/solution.py
@@ -88,7 +88,8 @@
         outer_pre = jnp.dot(inner_act, mid_weight, preferred_element_type=jnp.float32) + mid_bias
         return (inner_pre, outer_pre)
 
-    grouped = lax.all_gather(conf_src, "cfg", axis=0, tiled=True)
+    stack = jnp.stack([conf_src] * lax.axis_size("cfg"))
+    grouped = jnp.concatenate(lax.all_to_all(stack, "cfg", 0, 0), axis=0)
     spread = lax.all_to_all(
         grouped.reshape(group_count, node_count, per_peer, feat_width),
         "node",

time: 485 us -> 485 us (level)
    all_to_all x0 -> x1, blocking collectives: none -> 14.7 us  [shards(): grouped = jnp.concatenate(lax.all_to_all(stack, 'cfg', 0, 0), axis=0)]
    all_gather x1 -> x0, blocking collectives: 13.6 us -> none  [shards(): grouped = lax.all_gather(conf_src, 'cfg', axis=0, tiled=True)]
where the time goes in v1:
time: 485 us; the launch traced here: 480 us
  matrix products  132 us (27%)
  local copies, waits for them, and re-layouts  127 us (26%)
  blocking collectives  97.9 us (20%)
  waiting for transfers between devices  51.3 us (11%)
  starting transfers between devices  29.7 us (6%)
  between operations  16.9 us (3%)
  other arithmetic  14 us (3%)
  loops' own time  11.2 us (2%)
    psum x1, blocking collectives, shards(): local_score = lax.psum(partial_sums, 'node') * norm_scale  70.8 us
    gather x4, local copies, waits for them, and re-layouts, shards(): jnp.take(padded, neighbors[:, neighbor], axis=0).astype(jnp.float32)  67.7 us
    dot_general x16, matrix products, hidden_rows(): jnp.dot(inner_act, mid_weight, preferred_element_type=jnp.float32)  40 us
    dot_general x16, matrix products, config_total(): jnp.dot(jax.nn.silu(outer_pre), score_weight, precision=lax.Precision.HIG...  38.7 us
    dot_general x16, matrix products, config_step(): lax.dot_general(outer_grad, mid_weight, (((1,), (1,)), ((), ())), preferr...  33.9 us
    reduce_scatter x1, waiting for transfers between devices, shards(): lax.psum_scatter(group_part.astype(jnp.bfloat16), 'cfg', scatter_dimensio...  28.7 us
    dynamic_slice x32, local copies, waits for them, and re-layouts, shards(): partial_sums = lax.map(config_total, layout_ids)  24.5 us
    all_to_all x1, waiting for transfers between devices, shards(): lax.all_to_all(grouped.reshape(group_count, node_count, per_peer, feat_wi...  15 us
  transfers between devices with their start and end apart: 5, of which 4 were waited for; matrix products, arithmetic and copies ran while one was open for 2% of the time, Pallas kernels for 0%

profile of v1, /device:TPU:2, one launch (start us, length us, event | category | flops | bytes accessed | tf_op | source)
XLA Modules:
  0.0 480.3 jit_solution(6353628002819623985)
XLA Ops:
  8.3 3.4 collective-permute-start
  16.6 4.4 fusion.62
  21.4 17.0 %gather_fusion.4 = bf16[4096,256]{1,0:T(8,128)(2,1)} fusion(bf16[5120,256]{1,0:T(8,128)(2,1)S(1)} %constant_dynamic-update-slice_fusion, s32[4096]{0:T(1024)S(1)} %fusion.55), kind=kCustom, calls=%fused_computation.4.clone | custom fusion | bytes 4210688 | tf_op jit(solution)/shard_map/jit(_take)/gather | solution.py:65
  38.4 16.9 %gather_fusion.1 = bf16[4096,256]{1,0:T(8,128)(2,1)} fusion(bf16[5120,256]{1,0:T(8,128)(2,1)S(1)} %constant_dynamic-update-slice_fusion, s32[4096]{0:T(1024)S(1)} %fusion.52), kind=kCustom, calls=%fused_computation.clone | custom fusion | bytes 4210688 | tf_op jit(solution)/shard_map/jit(_take)/gather | solution.py:65
  55.3 16.9 %gather_fusion.2 = bf16[4096,256]{1,0:T(8,128)(2,1)} fusion(bf16[5120,256]{1,0:T(8,128)(2,1)S(1)} %constant_dynamic-update-slice_fusion, s32[4096]{0:T(1024)S(1)} %fusion.53), kind=kCustom, calls=%fused_computation.2.clone | custom fusion | bytes 4210688 | tf_op jit(solution)/shard_map/jit(_take)/gather | solution.py:65
  72.2 16.9 %gather_fusion.3 = bf16[4096,256]{1,0:T(8,128)(2,1)} fusion(bf16[5120,256]{1,0:T(8,128)(2,1)S(1)} %constant_dynamic-update-slice_fusion, s32[4096]{0:T(1024)S(1)} %fusion.54), kind=kCustom, calls=%fused_computation.3.clone | custom fusion | bytes 4210688 | tf_op jit(solution)/shard_map/jit(_take)/gather | solution.py:65
  89.1 8.0 %multiply_convert_fusion.5 = bf16[4096,256]{1,0:T(8,128)(2,1)S(1)} fusion(f32[4096,256]{1,0:T(8,128)} %fusion.62, bf16[256,256]{1,0:T(8,128)(2,1)S(1)} %copy-done.8, bf16[4096,256]{1,0:T(8,128)(2,1)} %gather_fusion.4, bf16[4096,256]{1,0:T(8,128)(2,1)} %gather_fusion.3, bf16[4096,256]{1,0:T(8,128)(2,1)} %gather_fusion.2, ...), kind=kOutput, calls=%fused_computation.48 | convolution fusion | flops 557842432 | bytes 14828544 | tf_op jit(solution)/shard_map/dot_general | solution.py:69
  98.2 14.7 %all_to_all.15 = bf16[8,128,256]{2,1,0:T(8,128)(2,1)S(1)} all-to-all(bf16[8,128,256]{2,1,0:T(8,128)(2,1)S(1)} %stack.2), channel_id=1, replica_groups=mesh['cfg'=8,'node'=32] {'cfg'}, dimensions={0} | all-to-all | bytes 1048576 | tf_op jit(solution)/shard_map/all_to_all | solution.py:92
  114.2 13.7 %all-to-all-start.1 = ((bf16[8,32,4,256]{3,2,0,1:T(4,128)(2,1)}), bf16[8,32,4,256]{3,2,0,1:T(4,128)(2,1)S(1)}, u32[]{:S(2)}, u32[]{:S(2)}) async-start(bf16[8,32,4,256]{3,2,0,1:T(4,128)(2,1)} %copy.20), calls=%async_computation.1 | async-start | bytes 1048576 | tf_op jit(solution)/shard_map/all_to_all | solution.py:93
  129.3 15.0 %all-to-all-done.1 = bf16[8,32,4,256]{3,2,0,1:T(4,128)(2,1)S(1)} async-done(((bf16[8,32,4,256]{3,2,0,1:T(4,128)(2,1)}), bf16[8,32,4,256]{3,2,0,1:T(4,128)(2,1)S(1)}, u32[]{:S(2)}, u32[]{:S(2)}) %all-to-all-start.1) | async-done | bytes 524320 | tf_op jit(solution)/shard_map/all_to_all | solution.py:93
  145.0 113.5 %while.22 = (s32[]{:T(128)}, f32[16]{0:T(128)S(1)}, s32[16,1024]{1,0:T(8,128)}, bf16[128,256]{1,0:T(8,128)(2,1)S(1)}, f32[1024,256]{1,0:T(8,128)S(1)}, /*index=5...) while((s32[]{:T(128)}, f32[16]{0:T(128)S(1)}, ...), condition=%wide.region_2.4_spmd.clone, body=%wide.region_0.3_spmd.clone.sunk | while | flops 207750144 | bytes 3366021 | solution.py:109
  152.9 2.5 convolution_add_fusion.6
  167.1 2.5 convolution_add_fusion.6
  188.4 2.5 convolution_add_fusion.6
  202.6 2.5 convolution_add_fusion.6
  216.8 2.5 convolution_add_fusion.6
  258.6 70.8 %psum.7 = f32[16]{0:T(128)S(1)} all-reduce(f32[16]{0:T(128)S(1)} %get-tuple-element.114), channel_id=1, replica_groups=mesh['cfg'=8,'node'=32] {'node'}, use_global_device_ids=true, to_apply=%region_3.5 | all-reduce | flops 16 | bytes 128 | tf_op jit(solution)/shard_map/psum | solution.py:110
  329.5 12.4 %all-reduce = f32[128]{0:T(128)S(1)} all-reduce(f32[128]{0:T(128)S(1)} %multiply_dynamic-update-slice_fusion), channel_id=1, replica_groups=mesh['cfg'=8,'node'=32] {'cfg'}, use_global_device_ids=true, to_apply=%add | all-reduce | flops 128 | bytes 1024
  341.9 3.3 gather_fusion.5
  345.2 3.3 gather_fusion.6
  349.1 72.5 %while.23 = (s32[]{:T(128)}, f32[1024,256]{1,0:T(8,128)S(1)}, f32[16]{0:T(128)S(1)}, f32[256]{0:T(256)S(1)}, s32[16,1024]{1,0:T(8,128)}, /*index=5*/bf16[128,256...) while((s32[]{:T(128)}, f32[1024,256]{1,0:T(8,128)S(1)}, ...), condition=%wide.region_6.9_spmd.clone, body=%wide.region_5.8_spmd.clone.sunk | while | flops 342753536 | bytes 5457063 | solution.py:129
  422.4 28.7 %reduce-scatter.2.cloned.1.call-done = bf16[128,256]{1,0:T(8,128)(2,1)} async-done(((bf16[1024,256]{1,0:T(8,128)(2,1)}), bf16[128,256]{1,0:T(8,128)(2,1)}) %reduce-scatter.2.cloned.1.call-update) | async-done | bytes 65552 | tf_op jit(solution)/shard_map/reduce_scatter | solution.py:130
  452.8 10.1 %all-to-all-start.2 = ((bf16[32,4,256]{2,1,0:T(4,128)(2,1)}), bf16[32,4,256]{2,1,0:T(4,128)(2,1)S(1)}, u32[]{:S(2)}, u32[]{:S(2)}) async-start(bf16[32,4,256]{2,1,0:T(4,128)(2,1)} %convert_element_type.55), calls=%async_computation.3 | async-start | bytes 131072 | tf_op jit(solution)/shard_map/all_to_all | solution.py:136
  464.2 7.4 %all-to-all-done.2 = bf16[32,4,256]{2,1,0:T(4,128)(2,1)S(1)} async-done(((bf16[32,4,256]{2,1,0:T(4,128)(2,1)}), bf16[32,4,256]{2,1,0:T(4,128)(2,1)S(1)}, u32[]{:S(2)}, u32[]{:S(2)}) %all-to-all-start.2) | async-done | bytes 65568 | tf_op jit(solution)/shard_map/all_to_all | solution.py:136
  (223 shorter events, 176.7 us)
Async XLA Ops:
  7.2 9.4 %copy-start = (bf16[256,256]{1,0:T(8,128)(2,1)S(1)}, bf16[256,256]{1,0:T(8,128)(2,1)}, u32[]{:S(2)}) copy-start(bf16[256,256]{1,0:T(8,128)(2,1)} %param.24) | copy-start | bytes 393220
  8.3 12.8 %collective-permute-start = (bf16[512,256]{1,0:T(8,128)(2,1)S(1)}, bf16[512,256]{1,0:T(8,128)(2,1)S(1)}, u32[]{:S(2)}, u32[]{:S(2)}) collective-permute-start(bf16[512,256]{1,0:T(8,128)(2,1)S(1)} %get-tuple-element.212), channel_id=1, source_target_pairs={{0,1},{1,2},{2,3},{3,4},{4,5},{5,6},{6,7},{7,8},{8,9},{9,10},{10,1... | collective-permute-start | bytes 786440 | tf_op jit(solution)/shard_map/ppermute | solution.py:17
  11.7 9.7 %collective-permute-start.1 = (bf16[512,256]{1,0:T(8,128)(2,1)S(1)}, bf16[512,256]{1,0:T(8,128)(2,1)S(1)}, u32[]{:S(2)}, u32[]{:S(2)}) collective-permute-start(bf16[512,256]{1,0:T(8,128)(2,1)S(1)} %get-tuple-element.211), channel_id=1, source_target_pairs={{1,0},{2,1},{3,2},{4,3},{5,4},{6,5},{7,6},{8,7},{9,8},{10,9},{11,1... | collective-permute-start | bytes 786440 | tf_op jit(solution)/shard_map/ppermute | solution.py:18
  16.6 4.5 copy-start.1
  72.2 16.9 %copy-start.8 = (bf16[256,256]{1,0:T(8,128)(2,1)S(1)}, bf16[256,256]{1,0:T(8,128)(2,1)}, u32[]{:S(2)}) copy-start(bf16[256,256]{1,0:T(8,128)(2,1)} %param.25) | copy-start | bytes 393220
  72.2 16.9 %copy-start.9 = (f32[256]{0:T(256)S(1)}, f32[256]{0:T(256)}, u32[]{:S(2)}) copy-start(f32[256]{0:T(256)} %param.26) | copy-start | bytes 3076
  97.2 17.0 %copy-start.4 = (bf16[4096,256]{1,0:T(8,128)(2,1)}, bf16[4096,256]{1,0:T(8,128)(2,1)S(1)}, u32[]{:S(2)}) copy-start(bf16[4096,256]{1,0:T(8,128)(2,1)S(1)} %multiply_convert_fusion.5) | copy-start | bytes 6291460
  98.2 29.8 %copy-start.11 = (u32[256]{0:T(256)S(1)}, u32[256]{0:T(256)}, u32[]{:S(2)}) copy-start(u32[256]{0:T(256)} %constant.97) | copy-start | bytes 3076
  98.2 31.1 %copy-start.7 = (s32[512,2]{0,1:T(2,128)S(1)}, s32[512,2]{0,1:T(2,128)}, u32[]{:S(2)}) copy-start(s32[512,2]{0,1:T(2,128)} %param.35) | copy-start | bytes 12292
  113.2 31.5 %copy-start.3 = (bf16[256,256]{1,0:T(8,128)(2,1)S(1)}, bf16[256,256]{1,0:T(8,128)(2,1)}, u32[]{:S(2)}) copy-start(bf16[256,256]{1,0:T(8,128)(2,1)} %param.29) | copy-start | bytes 393220
  114.2 30.1 %all-to-all-start.1 = ((bf16[8,32,4,256]{3,2,0,1:T(4,128)(2,1)}), bf16[8,32,4,256]{3,2,0,1:T(4,128)(2,1)S(1)}, u32[]{:S(2)}, u32[]{:S(2)}) async-start(bf16[8,32,4,256]{3,2,0,1:T(4,128)(2,1)} %copy.20), calls=%async_computation.1 | async-start | bytes 1048576 | tf_op jit(solution)/shard_map/all_to_all | solution.py:93
  127.9 17.1 %copy-start.2 = (bf16[128,256]{1,0:T(8,128)(2,1)S(1)}, bf16[128,256]{1,0:T(8,128)(2,1)}, u32[]{:S(2)}) copy-start(bf16[128,256]{1,0:T(8,128)(2,1)} %param.30) | copy-start | bytes 196612
  127.9 17.1 %copy-start.5 = (f32[256]{0:T(256)S(1)}, f32[256]{0:T(256)}, u32[]{:S(2)}) copy-start(f32[256]{0:T(256)} %param.31) | copy-start | bytes 3076
  127.9 17.1 %copy-start.6 = (f32[256]{0:T(256)S(1)}, f32[256]{0:T(256)}, u32[]{:S(2)}) copy-start(f32[256]{0:T(256)} %param.34) | copy-start | bytes 3076
  127.9 17.1 %copy-start.10 = (f32[256]{0:T(256)S(1)}, f32[256]{0:T(256)}, u32[]{:S(2)}) copy-start(f32[256]{0:T(256)} %param.33) | copy-start | bytes 3076
  127.9 323.2 %reduce-scatter.2.cloned.1.call-start = ((), (), s32[]{:S(2)}) async-start(), calls=%async_computation.4 | async-start | bytes 589824 | tf_op jit(solution)/shard_map/reduce_scatter | solution.py:130
  452.8 18.8 %all-to-all-start.2 = ((bf16[32,4,256]{2,1,0:T(4,128)(2,1)}), bf16[32,4,256]{2,1,0:T(4,128)(2,1)S(1)}, u32[]{:S(2)}, u32[]{:S(2)}) async-start(bf16[32,4,256]{2,1,0:T(4,128)(2,1)} %convert_element_type.55), calls=%async_computation.3 | async-start | bytes 131072 | tf_op jit(solution)/shard_map/all_to_all | solution.py:136
Sparse Core Ops, SparseCore 0:
  422.6 28.5 reduce-scatter.1
